TPU v7x, 32 devices: a whole 2x2x4 slice. The times are simulated.
32 devices in a mesh: groups: 2 (over y), dp: 4 (over x, core), tensor: 4 (over z).
Axes of the slice: x: 2, y: 2, z: 4, core: 2. Of those that a mesh axis runs over, the one named last changes fastest.
Arguments:
- query: bfloat16 [4096, 512], P(('groups', 'dp'), 'tensor'), parts along dimension 0, may hold values from -4.5 to 4.5
- keys: bfloat16 [4096, 512], P(('groups', 'dp'), 'tensor'), parts along dimension 0, may hold values from -4.5 to 4.5
- values: bfloat16 [4096, 512], P(('groups', 'dp'), 'tensor'), parts along dimension 0, may hold values from -6 to 6
- upstream: bfloat16 [4096, 8192], P(('groups', 'dp', 'tensor')), parts along dimension 0, may hold values from -6 to 6
- projection: bfloat16 [512, 8192], P('tensor', 'dp'), may hold values from -0.0625 to 0.0625
- lengths: int32 [8, 8], P(('groups', 'dp')), parts along dimension 0, may hold values from 1 to 256, 512 in all within a row
Outputs:
- grad_query: bfloat16 [4096, 512], P(('groups', 'dp'), 'tensor'), parts along dimension 0
- grad_keys: bfloat16 [4096, 512], P(('groups', 'dp'), 'tensor'), parts along dimension 0
- grad_values: bfloat16 [4096, 512], P(('groups', 'dp'), 'tensor'), parts along dimension 0
- grad_projection: float32 [1024, 8192], P(('groups', 'tensor'), 'dp'), parts along dimension 0
There are 2 independent parts, one for each index of `groups`. A program takes and returns all parts, laid end to end along the dimension named above; an argument that names none is the same for every part. Nothing has to cross between parts.
Inputs may be any that keep to these rules, and one draw needn't show every extreme that they name: Each row holds the lengths of the 8 documents of one sequence in order; they sum to 512 and the largest is exactly 256.
All inputs are finite; a program needn't handle non-finite values.
Results may differ from a plain program's by a relative error of at most 0.014.
Values may be sent and summed in bfloat16 or wider, within the bound.
No kernel may reach another device: no remote copies, remote signals or barrier semaphores. Data moves between devices by JAX's collectives and lax.ppermute only.
A program may use at most 64 MiB of HBM per device.

v0:
```python
import jax
import jax.numpy as jnp
from jax import lax
from jax.sharding import PartitionSpec as P

HD = 128


def sequence_mask(length_row, row_count):
    segment_ends = jnp.cumsum(length_row)
    places = jnp.arange(row_count, dtype=jnp.int32)
    labels = jnp.sum((segment_ends[None, :] <= places[:, None]).astype(jnp.int32), axis=1)
    same = labels[:, None] == labels[None, :]
    return jnp.logical_and(same, places[None, :] <= places[:, None])


def shards(query, keys, values, upstream, projection, lengths):
    row_count, width = query.shape
    head_count = width // HD
    scaling = HD ** (-0.5)
    allowed = sequence_mask(lengths[0], row_count)
    query_heads = query.reshape(row_count, head_count, HD)
    key_heads = keys.reshape(row_count, head_count, HD)
    value_heads = values.reshape(row_count, head_count, HD)
    scores = (
        jnp.einsum("qhd,khd->hqk", query_heads, key_heads, preferred_element_type=jnp.float32)
        * scaling
    )
    scores = jnp.where(allowed[None], scores, -1e30)
    row_max = jnp.max(scores, axis=2, keepdims=True)
    exponent = jnp.exp(scores - row_max)
    probs = exponent / jnp.sum(exponent, axis=2, keepdims=True)
    probs_low = probs.astype(jnp.bfloat16)
    attended = jnp.einsum(
        "hqk,khd->qhd", probs_low, value_heads, preferred_element_type=jnp.float32
    )
    attended = attended.astype(jnp.bfloat16).reshape(row_count, width)
    full_projection = lax.all_gather(projection, "dp", axis=1, tiled=True)
    gathered = lax.all_gather(upstream, "tensor", axis=0, tiled=True)
    out_total = lax.dot_general(
        gathered, full_projection, (((1,), (1,)), ((), ())), preferred_element_type=jnp.float32
    )
    partial_grad = lax.dot_general(
        attended, gathered, (((0,), (0,)), ((), ())), preferred_element_type=jnp.float32
    )
    grad_projection = lax.psum_scatter(
        partial_grad.astype(jnp.bfloat16), "dp", scatter_dimension=1, tiled=True
    ).astype(jnp.float32)
    out_grad = out_total.astype(jnp.bfloat16)
    grad_heads = out_grad.reshape(row_count, head_count, HD)
    grad_values = jnp.einsum(
        "hqk,qhd->khd", probs_low, grad_heads, preferred_element_type=jnp.float32
    ).astype(jnp.bfloat16)
    grad_probs = jnp.einsum(
        "qhd,khd->hqk", grad_heads, value_heads, preferred_element_type=jnp.float32
    )
    delta = jnp.sum(probs * grad_probs, axis=2, keepdims=True)
    grad_scores = (probs * (grad_probs - delta) * scaling).astype(jnp.bfloat16)
    grad_query = jnp.einsum(
        "hqk,khd->qhd", grad_scores, key_heads, preferred_element_type=jnp.float32
    ).astype(jnp.bfloat16)
    grad_keys = jnp.einsum(
        "hqk,qhd->khd", grad_scores, query_heads, preferred_element_type=jnp.float32
    ).astype(jnp.bfloat16)
    return (
        grad_query.reshape(row_count, width),
        grad_keys.reshape(row_count, width),
        grad_values.reshape(row_count, width),
        grad_projection,
    )


def solution(mesh):
    in_specs = (
        P(("groups", "dp"), "tensor"),
        P(("groups", "dp"), "tensor"),
        P(("groups", "dp"), "tensor"),
        P(("groups", "dp", "tensor"), None),
        P("tensor", "dp"),
        P(("groups", "dp"), None),
    )
    out_specs = (
        P(("groups", "dp"), "tensor"),
        P(("groups", "dp"), "tensor"),
        P(("groups", "dp"), "tensor"),
        P(("groups", "tensor"), "dp"),
    )
    return jax.shard_map(shards, mesh=mesh, in_specs=in_specs, out_specs=out_specs, check_vma=False)
```

profile of v0, /device:TPU:0, one launch (start us, length us, event | category | flops | bytes accessed | tf_op | source)
XLA Modules:
  0.0 226.7 jit_solution(17024745603641305551)
XLA Ops:
  7.2 0.0 copy-start
  7.2 0.0 all-gather.3.cloned.1.call-start
  7.2 0.7 all-gather.3.cloned.1.call-update
  7.9 0.0 all-gather.5.cloned.1.call-start
  8.0 0.7 all-gather.5.cloned.1.call-update
  8.7 0.0 reduce-scatter.2.cloned.1.call-start
  8.7 0.8 reduce-window.8
  9.5 0.1 convert_reduce_fusion
  9.6 1.3 fusion.11
  10.9 0.2 fusion.4
  11.1 150.8 %all-gather.3.cloned.1.call-done = bf16[512,8192]{1,0:T(8,128)(2,1)} async-done(((bf16[128,8192]{1,0:T(8,128)(2,1)}), bf16[512,8192]{1,0:T(8,128)(2,1)}) %all-gather.3.cloned.1.call-update) | async-done | bytes 8388624 | tf_op jit(solution)/shard_map/all_gather | solution.py:39
  161.9 0.0 copy-done
  161.9 6.5 %convolution_convert_fusion = bf16[128,8192]{1,0:T(8,128)(2,1)} fusion(bf16[512,8192]{1,0:T(8,128)(2,1)} %all-gather.3.cloned.1.call-done, bf16[512,128]{1,0:T(8,128)(2,1)S(1)} %copy-done, f32[512,512]{0,1:T(8,128)S(1)} %get-tuple-element.13, f32[512]{0:T(512)S(1)} %fusion.4, f32[512]{0:T(512)S(1)} %get-tuple-element.12), kind=kOutput, calls=%fused_computation | convolution fusion | flops 1142751232 | bytes 11669504 | tf_op jit(solution)/shard_map/dot_general | solution.py:43
  168.4 0.0 reduce-scatter.2.cloned.1.call-update
  168.4 15.8 %all-gather.5.cloned.1.call-done = bf16[128,8192]{1,0:T(8,128)(2,1)} async-done(((bf16[128,2048]{1,0:T(8,128)(2,1)}), bf16[128,8192]{1,0:T(8,128)(2,1)}) %all-gather.5.cloned.1.call-update) | async-done | bytes 2097168 | tf_op jit(solution)/shard_map/all_gather | solution.py:38
  184.3 6.3 %convolution_convert_fusion.5 = bf16[512,128]{1,0:T(8,128)(2,1)S(1)} fusion(bf16[512,8192]{1,0:T(8,128)(2,1)} %all-gather.3.cloned.1.call-done, bf16[128,8192]{1,0:T(8,128)(2,1)} %all-gather.5.cloned.1.call-done), kind=kOutput, calls=%fused_computation.7 | convolution fusion | flops 1073807360 | bytes 10616832 | tf_op jit(solution)/shard_map/dot_general | solution.py:40
  190.6 0.3 fusion.1
  190.9 0.0 copy-start.1
  190.9 0.0 copy-start.2
  191.0 0.8 copy.11
  191.7 0.3 multiply_reduce_fusion
  192.0 0.3 multiply_convert_fusion
  192.3 0.0 copy-done.1
  192.3 1.0 convolution_convert_fusion.3
  193.3 0.0 copy-done.2
  193.3 1.0 convolution_convert_fusion.4
  194.3 23.7 %reduce-scatter.2.cloned.1.call-done = bf16[128,2048]{1,0:T(8,128)(2,1)} async-done(((bf16[128,8192]{1,0:T(8,128)(2,1)}), bf16[128,2048]{1,0:T(8,128)(2,1)}) %reduce-scatter.2.cloned.1.call-update) | async-done | bytes 524304 | tf_op jit(solution)/shard_map/reduce_scatter | solution.py:46
  218.0 2.1 convert_element_type.58
Async XLA Ops:
  7.2 154.8 %copy-start = (bf16[512,128]{1,0:T(8,128)(2,1)S(1)}, bf16[512,128]{1,0:T(8,128)(2,1)}, u32[]{:S(2)}) copy-start(bf16[512,128]{1,0:T(8,128)(2,1)} %param.8) | copy-start | bytes 393220
  7.2 154.7 %all-gather.3.cloned.1.call-start = ((), (), s32[]{:S(2)}) async-start(), calls=%async_computation.1 | async-start | bytes 10485760 | tf_op jit(solution)/shard_map/all_gather | solution.py:39
  7.9 176.4 %all-gather.5.cloned.1.call-start = ((), (), s32[]{:S(2)}) async-start(), calls=%async_computation.2 | async-start | bytes 2621440 | tf_op jit(solution)/shard_map/all_gather | solution.py:38
  8.7 209.3 %reduce-scatter.2.cloned.1.call-start = ((), (), s32[]{:S(2)}) async-start(), calls=%async_computation.3 | async-start | bytes 2621440 | tf_op jit(solution)/shard_map/reduce_scatter | solution.py:46
  190.9 1.4 copy-start.1
  190.9 2.4 %copy-start.2 = (bf16[512,128]{1,0:T(8,128)(2,1)S(1)}, bf16[512,128]{1,0:T(8,128)(2,1)}, u32[]{:S(2)}) copy-start(bf16[512,128]{1,0:T(8,128)(2,1)} %param.7) | copy-start | bytes 393220
Sparse Core Ops, SparseCore 0:
  9.6 152.3 all-gather.2
  163.5 20.7 all-gather.4
  186.8 31.1 reduce-scatter.1
where the time goes:
time: 227 us
  waiting for transfers between devices  192 us (85%)
  matrix products  16.7 us (7%)
  between operations  13.8 us (6%)
  other arithmetic  3.53 us (2%)
    all_gather x1, waiting for transfers between devices, shards(): gathered = lax.all_gather(upstream, 'tensor', axis=0, tiled=True)  151 us
    reduce_scatter x1, waiting for transfers between devices, shards(): lax.psum_scatter(partial_grad.astype(jnp.bfloat16), 'dp', scatter_dimensi...  23.7 us
    all_gather x1, waiting for transfers between devices, shards(): full_projection = lax.all_gather(projection, 'dp', axis=1, tiled=True)  15.8 us
    dot_general x1, matrix products, shards(): lax.dot_general(attended, gathered, (((0,), (0,)), ((), ())), preferred_e...  6.48 us
    dot_general x1, matrix products, shards(): lax.dot_general(gathered, full_projection, (((1,), (1,)), ((), ())), pref...  6.31 us
  transfers between devices with their start and end apart: 3, of which 3 were waited for; matrix products, arithmetic and copies ran while one was open for 8% of the time, Pallas kernels for 0%

commit v1 on v0

--- a/solution.py
+++ b/solution.py
@@ -36,7 +36,9 @@
     )
     attended = attended.astype(jnp.bfloat16).reshape(row_count, width)
     full_projection = lax.all_gather(projection, "dp", axis=1, tiled=True)
-    gathered = lax.all_gather(upstream, "tensor", axis=0, tiled=True)
+    gathered = jnp.concatenate(
+        lax.all_to_all(jnp.stack([upstream] * lax.axis_size("tensor")), "tensor", 0, 0), axis=0
+    )
     out_total = lax.dot_general(
         gathered, full_projection, (((1,), (1,)), ((), ())), preferred_element_type=jnp.float32
     )

time: 227 us -> 250 us (1.10)
  waiting for transfers between devices: 192 us -> 204 us
  starting transfers between devices: 0.11 us -> 6.52 us
  local copies, waits for them, and re-layouts: 0.78 us -> 6.63 us
    all_to_all x0 -> x1, waiting for transfers between devices: none -> 182 us  [shards(): lax.all_to_all(jnp.stack([upstream] * lax.axis_size('tensor')), 'tensor',...]
    all_gather x1 -> x0, waiting for transfers between devices: 151 us -> none  [shards(): gathered = lax.all_gather(upstream, 'tensor', axis=0, tiled=True)]
    all_gather x1, waiting for transfers between devices: 15.8 us -> 0.02 us  [shards(): full_projection = lax.all_gather(projection, 'dp', axis=1, tiled=True)]
    all_to_all x0 -> x1, starting transfers between devices: none -> 6.48 us  [shards(): lax.all_to_all(jnp.stack([upstream] * lax.axis_size('tensor')), 'tensor',...]
    another operation x0 -> x1, local copies, waits for them, and re-layouts: none -> 5.85 us  [shards(): jnp.stack([upstream] * lax.axis_size('tensor'))]
    reduce_scatter x1, waiting for transfers between devices: 23.7 us -> 20.5 us  [shards(): lax.psum_scatter(partial_grad.astype(jnp.bfloat16), 'dp', scatter_dimensi...]
  transfers between devices with their start and end apart: 3 -> 3, of which waited for: 3 -> 2; matrix products, arithmetic and copies ran while one was open for 8% -> 7% of each run, Pallas kernels for 0% -> 0%
where the time goes in v1:
time: 250 us
  waiting for transfers between devices  204 us (82%)
  matrix products  15.9 us (6%)
  between operations  14.1 us (6%)
  local copies, waits for them, and re-layouts  6.63 us (3%)
  starting transfers between devices  6.52 us (3%)
  other arithmetic  2.87 us (1%)
    all_to_all x1, waiting for transfers between devices, shards(): lax.all_to_all(jnp.stack([upstream] * lax.axis_size('tensor')), 'tensor',...  182 us
    reduce_scatter x1, waiting for transfers between devices, shards(): lax.psum_scatter(partial_grad.astype(jnp.bfloat16), 'dp', scatter_dimensi...  20.5 us
    dot_general x1, matrix products, shards(): lax.dot_general(attended, gathered, (((0,), (0,)), ((), ())), preferred_e...  6.57 us
    all_to_all x1, starting transfers between devices, shards(): lax.all_to_all(jnp.stack([upstream] * lax.axis_size('tensor')), 'tensor',...  6.48 us
    dot_general x1, matrix products, shards(): lax.dot_general(gathered, full_projection, (((1,), (1,)), ((), ())), pref...  6.31 us
    another operation x1, local copies, waits for them, and re-layouts, shards(): jnp.stack([upstream] * lax.axis_size('tensor'))  5.85 us
  transfers between devices with their start and end apart: 3, of which 2 were waited for; matrix products, arithmetic and copies ran while one was open for 7% of the time, Pallas kernels for 0%

profile of v1, /device:TPU:0, one launch (start us, length us, event | category | flops | bytes accessed | tf_op | source)
XLA Modules:
  0.0 249.7 jit_solution(6975570248987011440)
XLA Ops:
  7.2 0.0 copy-start
  7.2 5.9 %stack.2 = bf16[4,128,8192]{2,1,0:T(8,128)(2,1)} broadcast(bf16[128,8192]{1,0:T(8,128)(2,1)} %param.9), dimensions={1,2} | broadcast | bytes 10485760 | tf_op jit(solution)/shard_map/stack | solution.py:40
  13.0 0.0 copy-start.3
  13.0 0.0 copy-start.1
  13.0 0.0 copy-start.2
  13.0 6.5 %all-to-all-start = ((bf16[4,128,8192]{2,1,0:T(8,128)(2,1)}), bf16[4,128,8192]{2,1,0:T(8,128)(2,1)}, u32[]{:S(2)}, u32[]{:S(2)}) async-start(bf16[4,128,8192]{2,1,0:T(8,128)(2,1)} %stack.2), calls=%async_computation | async-start | bytes 16777216 | tf_op jit(solution)/shard_map/all_to_all | solution.py:40
  19.5 0.0 all-gather.2.cloned.1.call-start
  19.5 0.7 all-gather.2.cloned.1.call-update
  20.2 0.0 reduce-scatter.2.cloned.1.call-start
  20.3 0.0 copy-done.3
  20.3 0.2 reduce-window.8
  20.5 0.1 convert_reduce_fusion
  20.6 0.0 copy-done.1
  20.6 0.0 copy-done.2
  20.6 0.4 fusion.11
  20.9 0.2 fusion.4
  21.1 182.5 %all-to-all-done = bf16[4,128,8192]{2,1,0:T(8,128)(2,1)} async-done(((bf16[4,128,8192]{2,1,0:T(8,128)(2,1)}), bf16[4,128,8192]{2,1,0:T(8,128)(2,1)}, u32[]{:S(2)}, u32[]{:S(2)}) %all-to-all-start) | async-done | bytes 8388640 | tf_op jit(solution)/shard_map/all_to_all | solution.py:40
  203.6 0.0 copy-done
  203.6 6.6 %convolution_convert_fusion = bf16[128,8192]{1,0:T(8,128)(2,1)} fusion(bf16[512,8192]{1,0:T(8,128)(2,1)} %bitcast.2, bf16[512,128]{1,0:T(8,128)(2,1)S(1)} %copy-done, f32[512,512]{0,1:T(8,128)S(1)} %get-tuple-element.13, f32[512]{0:T(512)S(1)} %fusion.4, f32[512]{0:T(512)S(1)} %get-tuple-element.12), kind=kOutput, calls=%fused_computation | convolution fusion | flops 1142751232 | bytes 11669504 | tf_op jit(solution)/shard_map/dot_general | solution.py:45
  210.2 0.0 reduce-scatter.2.cloned.1.call-update
  210.2 0.0 all-gather.2.cloned.1.call-done
  210.2 6.3 %convolution_convert_fusion.5 = bf16[512,128]{1,0:T(8,128)(2,1)S(1)} fusion(bf16[512,8192]{1,0:T(8,128)(2,1)} %bitcast.2, bf16[128,8192]{1,0:T(8,128)(2,1)} %all-gather.2.cloned.1.call-done), kind=kOutput, calls=%fused_computation.7 | convolution fusion | flops 1073807360 | bytes 10616832 | tf_op jit(solution)/shard_map/dot_general | solution.py:42
  216.6 0.3 fusion.1
  216.9 0.8 copy.11
  217.7 0.3 multiply_reduce_fusion
  218.0 0.3 multiply_convert_fusion
  218.3 1.0 convolution_convert_fusion.3
  219.2 1.0 convolution_convert_fusion.4
  220.2 20.5 %reduce-scatter.2.cloned.1.call-done = bf16[128,2048]{1,0:T(8,128)(2,1)} async-done(((bf16[128,8192]{1,0:T(8,128)(2,1)}), bf16[128,2048]{1,0:T(8,128)(2,1)}) %reduce-scatter.2.cloned.1.call-update) | async-done | bytes 524304 | tf_op jit(solution)/shard_map/reduce_scatter | solution.py:48
  240.7 2.1 convert_element_type.58
Async XLA Ops:
  7.2 196.4 %copy-start = (bf16[512,128]{1,0:T(8,128)(2,1)S(1)}, bf16[512,128]{1,0:T(8,128)(2,1)}, u32[]{:S(2)}) copy-start(bf16[512,128]{1,0:T(8,128)(2,1)} %param.8) | copy-start | bytes 393220
  13.0 7.3 %copy-start.3 = (s32[1,8]{1,0:T(1,128)S(1)}, s32[1,8]{1,0:T(1,128)}, u32[]{:S(2)}) copy-start(s32[1,8]{1,0:T(1,128)} %param.11) | copy-start | bytes 100
  13.0 7.5 %copy-start.1 = (bf16[512,128]{1,0:T(8,128)(2,1)S(1)}, bf16[512,128]{1,0:T(8,128)(2,1)}, u32[]{:S(2)}) copy-start(bf16[512,128]{1,0:T(8,128)(2,1)} %param.6) | copy-start | bytes 393220
  13.0 7.5 %copy-start.2 = (bf16[512,128]{1,0:T(8,128)(2,1)S(1)}, bf16[512,128]{1,0:T(8,128)(2,1)}, u32[]{:S(2)}) copy-start(bf16[512,128]{1,0:T(8,128)(2,1)} %param.7) | copy-start | bytes 393220
  13.0 190.6 %all-to-all-start = ((bf16[4,128,8192]{2,1,0:T(8,128)(2,1)}), bf16[4,128,8192]{2,1,0:T(8,128)(2,1)}, u32[]{:S(2)}, u32[]{:S(2)}) async-start(bf16[4,128,8192]{2,1,0:T(8,128)(2,1)} %stack.2), calls=%async_computation | async-start | bytes 16777216 | tf_op jit(solution)/shard_map/all_to_all | solution.py:40
  19.5 190.7 %all-gather.2.cloned.1.call-start = ((), (), s32[]{:S(2)}) async-start(), calls=%async_computation.2 | async-start | bytes 2621440 | tf_op jit(solution)/shard_map/all_gather | solution.py:38
  20.2 220.5 %reduce-scatter.2.cloned.1.call-start = ((), (), s32[]{:S(2)}) async-start(), calls=%async_computation.3 | async-start | bytes 2621440 | tf_op jit(solution)/shard_map/reduce_scatter | solution.py:48
Sparse Core Ops, SparseCore 0:
  21.9 24.7 all-gather.1
  210.3 30.3 reduce-scatter.1
